TPU v7x, 32 devices: a whole 2x2x4 slice. The times are simulated.
32 devices in a mesh: groups: 2 (over y), ctx: 4 (over z), dom: 2 (over x), tp: 2 (over core).
Axes of the slice: x: 2, y: 2, z: 4, core: 2. Of those that a mesh axis runs over, the one named last changes fastest.
Arguments:
- queries: bfloat16 [8, 32, 8, 8, 128], P('groups', 'dom', 'tp'), parts along dimension 0, may hold values from -8 to 8
- prompt_cache: bfloat16 [4, 8192, 8, 128], P('groups', 'ctx', 'tp'), parts along dimension 0, may hold values from -8 to 8
- suffix_cache: bfloat16 [4, 32, 16, 8, 128], P('groups', 'dom', 'ctx', 'tp'), parts along dimension 0, may hold values from -8 to 8
- new_kv: bfloat16 [8, 2, 32, 8, 128], P('groups', None, 'dom', 'tp'), parts along dimension 0, may hold values from -8 to 8
- ancestors: int32 [8, 32], P('groups'), parts along dimension 0, may hold values from 0 to 31, as said below
- lengths: int32 [64], P('groups'), parts along dimension 0, may hold values from 1 to 12, as said below
Outputs:
- attended: bfloat16 [8, 32, 8, 8, 128], P('groups', 'dom', 'tp'), parts along dimension 0
There are 2 independent parts, one for each index of `groups`. A program takes and returns all parts, laid end to end along the dimension named above; each array names one. Nothing has to cross between parts.
Inputs may be any that keep to these rules, and one draw needn't show every extreme that they name: `ancestors`: particle p is owned by owner p // 16. In every step, of the 16 offspring of one owner at most 16 have their ancestor among the particles of any one owner, and each owner has exactly 16 from some one owner. `lengths`: the largest length is reached in every draw.
All inputs are finite; a program needn't handle non-finite values.
Results may differ from a plain program's by a relative error of at most 0.005.
Values may be sent and summed in bfloat16 or wider, within the bound.
A program may use at most 128 MiB of HBM per device.

v0:
```python
import math
import jax
import jax.numpy as jnp
from jax import lax
from jax.sharding import PartitionSpec as P


def resample_whole(flat_rows, my_parents, particles):
    one_hot = (my_parents[:, None] == jnp.arange(particles, dtype=jnp.int32)[None, :]).astype(
        jnp.bfloat16
    )
    gathered = jnp.einsum(
        "ji,cir->cjr",
        one_hot,
        lax.all_gather(flat_rows, "dom", axis=1, tiled=True),
        preferred_element_type=jnp.float32,
    )
    return gathered.astype(jnp.bfloat16)


def attend(query_block, prompt_keys, prompt_values, suffix_rows, visible, score_scale):
    prompt_scores = (
        jnp.einsum("pkgh,tkh->kpgt", query_block, prompt_keys, preferred_element_type=jnp.float32)
        * score_scale
    )
    suffix_scores = (
        jnp.einsum(
            "pkgh,pskh->pkgs", query_block, suffix_rows[0], preferred_element_type=jnp.float32
        )
        * score_scale
    )
    suffix_scores = jnp.where(visible[:, None, None, :], suffix_scores, -jnp.inf)
    local_peak = jnp.maximum(
        jnp.transpose(jnp.max(prompt_scores, axis=-1), (1, 0, 2)), jnp.max(suffix_scores, axis=-1)
    )
    peak_score = lax.pmax(local_peak, "ctx")
    prompt_exp = jnp.exp(prompt_scores - jnp.transpose(peak_score, (1, 0, 2))[..., None])
    suffix_exp = jnp.exp(suffix_scores - peak_score[..., None])
    totals = jnp.transpose(jnp.sum(prompt_exp, axis=-1), (1, 0, 2)) + jnp.sum(suffix_exp, axis=-1)
    prompt_weights = prompt_exp.astype(jnp.bfloat16)
    suffix_weights = suffix_exp.astype(jnp.bfloat16)
    numerator = jnp.einsum(
        "kpgt,tkh->pkgh", prompt_weights, prompt_values, preferred_element_type=jnp.float32
    )
    numerator = numerator + jnp.einsum(
        "pkgs,pskh->pkgh", suffix_weights, suffix_rows[1], preferred_element_type=jnp.float32
    )
    total_all, numerator_all = lax.psum((totals, numerator), "ctx")
    return (numerator_all / total_all[..., None]).astype(jnp.bfloat16)


def on_device(queries, prompt_cache, suffix_cache, new_kv, ancestors, lengths):
    my_owner = lax.axis_index("dom")
    my_shard = lax.axis_index("ctx")
    per_owner = queries.shape[1]
    suffix_dev = suffix_cache.shape[2]
    particles = ancestors.shape[1]
    score_scale = 1.0 / math.sqrt(queries.shape[4])
    prompt_keys = prompt_cache[0]
    prompt_values = prompt_cache[1]
    particle_ids = jnp.arange(particles, dtype=jnp.int32)
    positions = my_shard * suffix_dev + jnp.arange(suffix_dev, dtype=jnp.int32)
    suffix_rows = suffix_cache
    lengths_now = lengths
    results = []
    for step_index in range(queries.shape[0]):
        parents = ancestors[step_index]
        my_parents = lax.dynamic_slice_in_dim(parents, my_owner * per_owner, per_owner)
        flat_rows = suffix_rows.reshape(2, per_owner, -1)
        moved_rows = resample_whole(flat_rows, my_parents, particles)
        suffix_rows = moved_rows.reshape(suffix_rows.shape)
        lengths_now = jnp.sum(
            jnp.where(parents[:, None] == particle_ids[None, :], lengths_now[None, :], 0), axis=1
        )
        my_lengths = lax.dynamic_slice_in_dim(lengths_now, my_owner * per_owner, per_owner)
        new_slot = positions[None, :] == my_lengths[:, None]
        suffix_rows = jnp.where(
            new_slot[None, :, :, None, None], new_kv[step_index][:, :, None], suffix_rows
        )
        visible = positions[None, :] <= my_lengths[:, None]
        results.append(
            attend(
                queries[step_index], prompt_keys, prompt_values, suffix_rows, visible, score_scale
            )
        )
        lengths_now = lengths_now + 1
    return jnp.stack(results)


def solution(mesh):
    return jax.shard_map(
        on_device,
        mesh=mesh,
        in_specs=(
            P("groups", "dom", "tp", None, None),
            P("groups", "ctx", "tp", None),
            P("groups", "dom", "ctx", "tp", None),
            P("groups", None, "dom", "tp", None),
            P("groups", None),
            P("groups"),
        ),
        out_specs=P("groups", "dom", "tp", None, None),
        check_vma=False,
    )
```

profile of v0, /device:TPU:0, one launch (start us, length us, event | category | flops | bytes accessed | tf_op | source)
XLA Modules:
  0.0 163.5 jit_solution(15562038349087660170)
XLA Ops:
  8.8 4.1 %fusion.100 = (bf16[1,2048,4,128]{3,2,1,0:T(4,128)(2,1)S(1)}, bf16[1,2048,4,128]{3,2,1,0:T(4,128)(2,1)}) fusion(bf16[2,2048,4,128]{3,2,1,0:T(4,128)(2,1)} %param.7), kind=kLoop, calls=%fused_computation.178 | loop fusion | bytes 8388608 | tf_op jit(solution)/shard_map/slice | solution.py:59
  17.0 7.1 %all_gather.12 = bf16[2,32,2048]{2,1,0:T(8,128)(2,1)S(1)} all-gather(bf16[2,16,2048]{2,1,0:T(8,128)(2,1)S(1)} %reshape.274), channel_id=1, replica_groups=mesh['groups'=2,'ctx'=4,'dom'=2,'tp'=2] {'dom'}, dimensions={1}, use_global_device_ids=true | all-gather | bytes 393216 | tf_op jit(solution)/shard_map/all_gather | solution.py:15
  24.4 5.6 %all_gather.13 = bf16[2,32,2048]{2,1,0:T(8,128)(2,1)S(1)} all-gather(bf16[2,16,2048]{2,1,0:T(8,128)(2,1)S(1)} %get-tuple-element.59), channel_id=1, replica_groups=mesh['groups'=2,'ctx'=4,'dom'=2,'tp'=2] {'dom'}, dimensions={1}, use_global_device_ids=true | all-gather | bytes 393216 | tf_op jit(solution)/shard_map/all_gather | solution.py:15
  30.4 5.6 %all_gather.14 = bf16[2,32,2048]{2,1,0:T(8,128)(2,1)S(1)} all-gather(bf16[2,16,2048]{2,1,0:T(8,128)(2,1)S(1)} %get-tuple-element.61), channel_id=1, replica_groups=mesh['groups'=2,'ctx'=4,'dom'=2,'tp'=2] {'dom'}, dimensions={1}, use_global_device_ids=true | all-gather | bytes 393216 | tf_op jit(solution)/shard_map/all_gather | solution.py:15
  36.3 5.8 %all_gather.15 = bf16[2,32,2048]{2,1,0:T(8,128)(2,1)S(1)} all-gather(bf16[2,16,2048]{2,1,0:T(8,128)(2,1)S(1)} %get-tuple-element.63), channel_id=1, replica_groups=mesh['groups'=2,'ctx'=4,'dom'=2,'tp'=2] {'dom'}, dimensions={1}, use_global_device_ids=true | all-gather | bytes 393216 | tf_op jit(solution)/shard_map/all_gather | solution.py:15
  42.5 4.1 %multiply_reduce_fusion = (f32[4,16,8]{2,1,0:T(8,128)}, f32[4,16,8,2048]{3,2,1,0:T(8,128)}) fusion(bf16[1,2048,4,128]{3,2,1,0:T(4,128)(2,1)S(1)} %get-tuple-element.17, bf16[1,16,4,8,128]{4,3,2,1,0:T(8,128)(2,1)} %get-tuple-element.22), kind=kOutput, calls=%fused_computation.4 | convolution fusion | flops 270532096 | bytes 6424576 | tf_op jit(solution)/shard_map/pkgh,tkh->kpgt/dot_general | solution.py:23
  46.7 3.3 %multiply_reduce_fusion.1 = (f32[4,16,8]{2,1,0:T(8,128)}, f32[4,16,8,2048]{3,2,1,0:T(8,128)}) fusion(bf16[1,2048,4,128]{3,2,1,0:T(4,128)(2,1)S(1)} %get-tuple-element.17, bf16[1,16,4,8,128]{4,3,2,1,0:T(8,128)(2,1)S(1)} %copy-done.10), kind=kOutput, calls=%fused_computation.5 | convolution fusion | flops 270532096 | bytes 6424576 | tf_op jit(solution)/shard_map/pkgh,tkh->kpgt/dot_general | solution.py:23
  50.0 3.3 %multiply_reduce_fusion.2 = (f32[4,16,8]{2,1,0:T(8,128)}, f32[4,16,8,2048]{3,2,1,0:T(8,128)}) fusion(bf16[1,2048,4,128]{3,2,1,0:T(4,128)(2,1)S(1)} %get-tuple-element.17, bf16[1,16,4,8,128]{4,3,2,1,0:T(8,128)(2,1)S(1)} %copy-done.9), kind=kOutput, calls=%fused_computation.6 | convolution fusion | flops 270532096 | bytes 6424576 | tf_op jit(solution)/shard_map/pkgh,tkh->kpgt/dot_general | solution.py:23
  53.5 2.7 %multiply_reduce_fusion.3 = (f32[4,16,8]{2,1,0:T(8,128)S(1)}, f32[4,16,8,2048]{3,2,1,0:T(8,128)}) fusion(bf16[1,2048,4,128]{3,2,1,0:T(4,128)(2,1)S(1)} %get-tuple-element.17, bf16[1,16,4,8,128]{4,3,2,1,0:T(8,128)(2,1)S(1)} %copy-done.8), kind=kOutput, calls=%fused_computation.7 | convolution fusion | flops 270532096 | bytes 6424576 | tf_op jit(solution)/shard_map/pkgh,tkh->kpgt/dot_general | solution.py:23
  56.2 1.1 copy_select_fusion
  57.3 1.6 fusion.102
  58.9 1.4 bitcast_maximum_fusion
  63.2 22.2 %all-reduce.2 = (f32[16,4,8]{2,0,1:T(8,128)S(1)}, f32[16,4,8]{2,0,1:T(8,128)S(1)}, f32[16,4,8]{2,0,1:T(8,128)S(1)}, f32[16,4,8]{2,0,1:T(8,128)S(1)}) all-reduce(f32[16,4,8]{2,0,1:T(8,128)} %bitcast_maximum_fusion, f32[16,4,8]{2,0,1:T(8,128)} %bitcast_maximum_fusion.1, ...), channel_id=1, replica_groups=mesh['groups'=2,'ctx'=4,'dom'=2,'tp'=2] {'ctx'}, use_global_device_ids=true, to_apply=%region_27.28 | all-reduce | flops 2048 | bytes 16384 | tf_op jit(solution)/shard_map/pmax | solution.py:36
  86.6 3.4 %fusion.41 = f32[16,4,8,128]{3,2,0,1:T(8,128)S(1)} fusion(bf16[1,2048,4,128]{3,2,1,0:T(4,128)(2,1)S(1)} %copy-done.6, f32[4,16,8,2048]{3,2,1,0:T(8,128)} %get-tuple-element.58, f32[4,16,8]{2,1,0:T(8,128)S(1)} %bitcast.214), kind=kOutput, calls=%fused_computation.49 | convolution fusion | flops 271581184 | bytes 6555648 | tf_op jit(solution)/shard_map/kpgt,tkh->pkgh/dot_general | solution.py:42
  91.0 1.1 fusion.38
  93.2 1.1 fusion.35
  95.4 1.1 fusion.32
  97.7 3.2 %fusion.6 = f32[4,16,8]{2,1,0:T(8,128)S(1)} fusion(f32[4,16,8,2048]{3,2,1,0:T(8,128)} %get-tuple-element.58, f32[4,16,8]{2,1,0:T(8,128)S(1)} %bitcast.215), kind=kLoop, calls=%fused_computation.14 | loop fusion | flops 3145216 | bytes 4198400 | tf_op jit(solution)/shard_map/reduce_sum | solution.py:39
  104.8 21.4 %all-reduce = (f32[16,4,8]{2,0,1:T(8,128)S(1)}, f32[16,4,8]{2,0,1:T(8,128)S(1)}, f32[16,4,8]{2,0,1:T(8,128)S(1)}, f32[16,4,8]{2,0,1:T(8,128)S(1)}) all-reduce(f32[16,4,8]{2,0,1:T(8,128)S(1)} %bitcast_add_fusion, f32[16,4,8]{2,0,1:T(8,128)S(1)} %bitcast_add_fusion.1, ...), channel_id=1, replica_groups=mesh['groups'=2,'ctx'=4,'dom'=2,'tp'=2] {'ctx'}, use_global_device_ids=true, to_apply=%region_31.32 | all-reduce | flops 2048 | bytes 16384 | tf_op jit(solution)/shard_map/psum | solution.py:48
  126.2 25.2 %all-reduce.5.cloned.1.call-done = (f32[16,4,8,128]{3,2,0,1:T(8,128)}, f32[16,4,8,128]{3,2,0,1:T(8,128)}, f32[16,4,8,128]{3,2,0,1:T(8,128)}, f32[16,4,8,128]{3,2,0,1:T(8,128)}) async-done(((f32[16,4,8,128]{3,2,0,1:T(8,128)}, f32[16,4,8,128]{3,2,0,1:T(8,128)}, f32[16,4,8,128]{3,2,0,1:T(8,128)}, f32[16,4,8,128]{3,2,0,1:T(8,128)}), (f32[16,4,8,128]{3,2,0,1:T(8,128)}, f32[16,4,8,128]{3,2,0,1:T(8,128)}, ...) | async-done | bytes 1048592 | tf_op jit(solution)/shard_map/psum | solution.py:48
  151.3 1.1 fusion.59
  152.4 1.1 fusion.58
  153.5 1.1 fusion.57
  154.6 1.1 fusion.56
  (115 shorter events, 21.1 us)
Async XLA Ops:
  6.5 144.8 %all-reduce.5.cloned.1.call-start = ((), (), s32[]{:S(2)}) async-start(), calls=%async_computation | async-start | bytes 2097152 | tf_op jit(solution)/shard_map/psum | solution.py:48
  8.8 4.1 %copy-start.7 = (bf16[4,16,4,8,128]{4,3,2,1,0:T(8,128)(2,1)S(1)}, bf16[4,16,4,8,128]{4,3,2,1,0:T(8,128)(2,1)}, u32[]{:S(2)}) copy-start(bf16[4,16,4,8,128]{4,3,2,1,0:T(8,128)(2,1)} %param.6) | copy-start | bytes 1572868
  8.8 4.9 %copy-start.18 = (bf16[4,2,16,4,128]{4,3,2,1,0:T(4,128)(2,1)S(1)}, bf16[4,2,16,4,128]{4,3,2,1,0:T(4,128)(2,1)}, u32[]{:S(2)}) copy-start(bf16[4,2,16,4,128]{4,3,2,1,0:T(4,128)(2,1)} %param.9) | copy-start | bytes 393220
  8.8 8.1 %copy-start.19 = (bf16[2,16,4,4,128]{4,3,2,1,0:T(4,128)(2,1)S(1)}, bf16[2,16,4,4,128]{4,3,2,1,0:T(4,128)(2,1)}, u32[]{:S(2)}) copy-start(bf16[2,16,4,4,128]{4,3,2,1,0:T(4,128)(2,1)} %param.8) | copy-start | bytes 393220
  14.4 0.6 copy-start.15
  14.4 2.2 %copy-start.11 = (bf16[2,16,4,128]{3,2,1,0:T(4,128)(2,1)}, bf16[2,16,4,128]{3,2,1,0:T(4,128)(2,1)S(1)}, u32[]{:S(2)}) copy-start(bf16[2,16,4,128]{3,2,1,0:T(4,128)(2,1)S(1)} %get-tuple-element.32) | copy-start | bytes 98308
  14.4 2.2 %copy-start.13 = (bf16[2,16,4,128]{3,2,1,0:T(4,128)(2,1)}, bf16[2,16,4,128]{3,2,1,0:T(4,128)(2,1)S(1)}, u32[]{:S(2)}) copy-start(bf16[2,16,4,128]{3,2,1,0:T(4,128)(2,1)S(1)} %get-tuple-element.33) | copy-start | bytes 98308
  36.3 10.4 %copy-start.10 = (bf16[1,16,4,8,128]{4,3,2,1,0:T(8,128)(2,1)S(1)}, bf16[1,16,4,8,128]{4,3,2,1,0:T(8,128)(2,1)}, u32[]{:S(2)}) copy-start(bf16[1,16,4,8,128]{4,3,2,1,0:T(8,128)(2,1)} %get-tuple-element.20) | copy-start | bytes 393220
  46.7 3.3 %copy-start.9 = (bf16[1,16,4,8,128]{4,3,2,1,0:T(8,128)(2,1)S(1)}, bf16[1,16,4,8,128]{4,3,2,1,0:T(8,128)(2,1)}, u32[]{:S(2)}) copy-start(bf16[1,16,4,8,128]{4,3,2,1,0:T(8,128)(2,1)} %get-tuple-element.21) | copy-start | bytes 393220
  50.0 3.5 %copy-start.8 = (bf16[1,16,4,8,128]{4,3,2,1,0:T(8,128)(2,1)S(1)}, bf16[1,16,4,8,128]{4,3,2,1,0:T(8,128)(2,1)}, u32[]{:S(2)}) copy-start(bf16[1,16,4,8,128]{4,3,2,1,0:T(8,128)(2,1)} %get-tuple-element.19) | copy-start | bytes 393220
  53.4 7.8 %copy-start.17 = (f32[4,16,8]{2,1,0:T(8,128)S(1)}, f32[4,16,8]{2,1,0:T(8,128)}, u32[]{:S(2)}) copy-start(f32[4,16,8]{2,1,0:T(8,128)} %get-tuple-element.67) | copy-start | bytes 6148
  53.5 8.4 %copy-start.12 = (bf16[2,16,4,128]{3,2,1,0:T(4,128)(2,1)S(1)}, bf16[2,16,4,128]{3,2,1,0:T(4,128)(2,1)}, u32[]{:S(2)}) copy-start(bf16[2,16,4,128]{3,2,1,0:T(4,128)(2,1)} %copy-done.11) | copy-start | bytes 98308
  53.5 8.4 %copy-start.14 = (bf16[2,16,4,128]{3,2,1,0:T(4,128)(2,1)S(1)}, bf16[2,16,4,128]{3,2,1,0:T(4,128)(2,1)}, u32[]{:S(2)}) copy-start(bf16[2,16,4,128]{3,2,1,0:T(4,128)(2,1)} %copy-done.13) | copy-start | bytes 98308
  53.5 8.6 %copy-start.21 = (pred[16,4]{1,0:T(8,128)(4,1)S(1)}, pred[16,4]{1,0:T(8,128)(4,1)}, u32[]{:S(2)}) copy-start(pred[16,4]{1,0:T(8,128)(4,1)} %get-tuple-element.52) | copy-start | bytes 196
  53.5 8.8 %copy-start.16 = (f32[4,16,8]{2,1,0:T(8,128)S(1)}, f32[4,16,8]{2,1,0:T(8,128)}, u32[]{:S(2)}) copy-start(f32[4,16,8]{2,1,0:T(8,128)} %get-tuple-element.71) | copy-start | bytes 6148
  53.5 9.5 %copy-start.20 = (pred[16,4]{1,0:T(8,128)(4,1)S(1)}, pred[16,4]{1,0:T(8,128)(4,1)}, u32[]{:S(2)}) copy-start(pred[16,4]{1,0:T(8,128)(4,1)} %get-tuple-element.43) | copy-start | bytes 196
  56.2 30.4 %copy-start.6 = (bf16[1,2048,4,128]{3,2,1,0:T(4,128)(2,1)S(1)}, bf16[1,2048,4,128]{3,2,1,0:T(4,128)(2,1)}, u32[]{:S(2)}) copy-start(bf16[1,2048,4,128]{3,2,1,0:T(4,128)(2,1)} %get-tuple-element.18) | copy-start | bytes 6291460
  86.6 4.4 %copy-start.2 = (f32[4,16,8,2048]{3,2,1,0:T(8,128)S(1)}, f32[4,16,8,2048]{3,2,1,0:T(8,128)}, u32[]{:S(2)}) copy-start(f32[4,16,8,2048]{3,2,1,0:T(8,128)} %get-tuple-element.68) | copy-start | bytes 12582916
  91.0 2.2 %copy-start.4 = (f32[4,16,8,2048]{3,2,1,0:T(8,128)S(1)}, f32[4,16,8,2048]{3,2,1,0:T(8,128)}, u32[]{:S(2)}) copy-start(f32[4,16,8,2048]{3,2,1,0:T(8,128)} %get-tuple-element.72) | copy-start | bytes 12582916
  93.2 2.2 %copy-start = (f32[4,16,8,2048]{3,2,1,0:T(8,128)S(1)}, f32[4,16,8,2048]{3,2,1,0:T(8,128)}, u32[]{:S(2)}) copy-start(f32[4,16,8,2048]{3,2,1,0:T(8,128)} %get-tuple-element.76) | copy-start | bytes 12582916
  97.7 3.5 %copy-start.3 = (f32[4,16,8,2048]{3,2,1,0:T(8,128)S(1)}, f32[4,16,8,2048]{3,2,1,0:T(8,128)}, u32[]{:S(2)}) copy-start(f32[4,16,8,2048]{3,2,1,0:T(8,128)} %get-tuple-element.68) | copy-start | bytes 12582916
  97.7 4.9 %copy-start.5 = (f32[4,16,8,2048]{3,2,1,0:T(8,128)S(1)}, f32[4,16,8,2048]{3,2,1,0:T(8,128)}, u32[]{:S(2)}) copy-start(f32[4,16,8,2048]{3,2,1,0:T(8,128)} %get-tuple-element.72) | copy-start | bytes 12582916
  101.1 2.8 %copy-start.1 = (f32[4,16,8,2048]{3,2,1,0:T(8,128)S(1)}, f32[4,16,8,2048]{3,2,1,0:T(8,128)}, u32[]{:S(2)}) copy-start(f32[4,16,8,2048]{3,2,1,0:T(8,128)} %get-tuple-element.76) | copy-start | bytes 12582916
Sparse Core Ops, SparseCore 0:
  97.8 53.5 all-reduce.4
where the time goes:
time: 164 us
  blocking collectives  67.7 us (41%)
  matrix products  27.9 us (17%)
  waiting for transfers between devices  25.2 us (15%)
  other arithmetic  17.6 us (11%)
  between operations  13.9 us (8%)
  local copies, waits for them, and re-layouts  11.3 us (7%)
    psum x1, waiting for transfers between devices, attend(): total_all, numerator_all = lax.psum((totals, numerator), 'ctx')  25.2 us
    all_gather x4, blocking collectives, resample_whole(): lax.all_gather(flat_rows, 'dom', axis=1, tiled=True)  24.2 us
    pmax x1, blocking collectives, attend(): peak_score = lax.pmax(local_peak, 'ctx')  22.2 us
    psum x1, blocking collectives, attend(): total_all, numerator_all = lax.psum((totals, numerator), 'ctx')  21.4 us
    dot_general x4, matrix products, attend(): jnp.einsum('pkgh,tkh->kpgt', query_block, prompt_keys, preferred_element_...  13.4 us
    dot_general x4, matrix products, attend(): jnp.einsum('kpgt,tkh->pkgh', prompt_weights, prompt_values, preferred_ele...  6.59 us
    reduce_sum x4, other arithmetic, attend(): jnp.sum(prompt_exp, axis=-1)  5.62 us
    another operation x5, other arithmetic, on_device(): return jnp.stack(results)  4.42 us
  transfers between devices with their start and end apart: 1, of which 1 were waited for; matrix products, arithmetic and copies ran while one was open for 3% of the time, Pallas kernels for 0%

commit v1 on v0

--- a/solution.py
+++ b/solution.py
@@ -3,18 +3,36 @@
 import jax.numpy as jnp
 from jax import lax
 from jax.sharding import PartitionSpec as P
+from jax.lax import axis_index, axis_size, ppermute
 
 
 def resample_whole(flat_rows, my_parents, particles):
     one_hot = (my_parents[:, None] == jnp.arange(particles, dtype=jnp.int32)[None, :]).astype(
         jnp.bfloat16
     )
+    heard = axis_size("dom")
+    left_arr = axis_index("dom")
+    all_rows, piece_next = (heard, left_arr)
+    pages = [(b, (b - 1) % all_rows) for b in range(all_rows)]
+    v1 = flat_rows.shape[1]
+    oldest = flat_rows
     gathered = jnp.einsum(
         "ji,cir->cjr",
-        one_hot,
-        lax.all_gather(flat_rows, "dom", axis=1, tiled=True),
+        lax.dynamic_slice_in_dim(one_hot, piece_next * v1, oldest.shape[1], axis=1),
+        oldest,
         preferred_element_type=jnp.float32,
     )
+    for c in range(1, all_rows):
+        oldest = ppermute(oldest, "dom", perm=pages)
+        low = jnp.einsum(
+            "ji,cir->cjr",
+            lax.dynamic_slice_in_dim(
+                one_hot, (piece_next + c) % all_rows * v1, oldest.shape[1], axis=1
+            ),
+            oldest,
+            preferred_element_type=jnp.float32,
+        )
+        gathered = gathered + low
     return gathered.astype(jnp.bfloat16)
 
 

time: 164 us -> 169 us (1.030)
  blocking collectives: 67.7 us -> 44.5 us
  waiting for transfers between devices: 25.2 us -> 35.7 us
  starting transfers between devices: 0.01 us -> 5.28 us
  local copies, waits for them, and re-layouts: 11.3 us -> 15.7 us
  matrix products: 27.9 us -> 32 us
  other arithmetic: 17.6 us -> 21.3 us
    all_gather x4 -> x0, blocking collectives: 24.2 us -> none  [resample_whole(): lax.all_gather(flat_rows, 'dom', axis=1, tiled=True)]
    ppermute x0 -> x4, waiting for transfers between devices: none -> 7.55 us  [resample_whole(): oldest = ppermute(oldest, 'dom', perm=pages)]
    ppermute x0 -> x4, starting transfers between devices: none -> 5.28 us  [resample_whole(): oldest = ppermute(oldest, 'dom', perm=pages)]
    dot_general x4 -> x8, matrix products: 0.92 us -> 4.55 us  [the longest x4 3.65 us: resample_whole(): jnp.einsum('ji,cir->cjr', lax.dynamic_slice_in_dim(one_hot, (piece_next +...]
    psum x1, waiting for transfers between devices: 25.2 us -> 28.1 us  [attend(): total_all, numerator_all = lax.psum((totals, numerator), 'ctx')]
    dot_general x4, matrix products: 6.59 us -> 4.25 us  [attend(): jnp.einsum('kpgt,tkh->pkgh', prompt_weights, prompt_values, preferred_ele...]
    reduce_sum x4, other arithmetic: 5.62 us -> 7.8 us  [attend(): jnp.sum(prompt_exp, axis=-1)]
    broadcast_in_dim x13, local copies, waits for them, and re-layouts: 1.51 us -> 3.31 us  [on_device(): jnp.where(new_slot[None, :, :, None, None], new_kv[step_index][:, :, None...]
  transfers between devices with their start and end apart: 1 -> 5, of which waited for: 1 -> 3; matrix products, arithmetic and copies ran while one was open for 3% -> 22% of each run, Pallas kernels for 0% -> 0%
where the time goes in v1:
time: 169 us; the launch traced here: 168 us
  blocking collectives  44.5 us (26%)
  waiting for transfers between devices  35.7 us (21%)
  matrix products  32 us (19%)
  other arithmetic  21.3 us (13%)
  local copies, waits for them, and re-layouts  15.7 us (9%)
  between operations  13.8 us (8%)
  starting transfers between devices  5.28 us (3%)
    psum x1, waiting for transfers between devices, attend(): total_all, numerator_all = lax.psum((totals, numerator), 'ctx')  28.1 us
    psum x1, blocking collectives, attend(): total_all, numerator_all = lax.psum((totals, numerator), 'ctx')  22.4 us
    pmax x1, blocking collectives, attend(): peak_score = lax.pmax(local_peak, 'ctx')  22.1 us
    dot_general x4, matrix products, attend(): jnp.einsum('pkgh,tkh->kpgt', query_block, prompt_keys, preferred_element_...  15 us
    reduce_sum x4, other arithmetic, attend(): jnp.sum(prompt_exp, axis=-1)  7.8 us
    ppermute x4, waiting for transfers between devices, resample_whole(): oldest = ppermute(oldest, 'dom', perm=pages)  7.55 us
    ppermute x4, starting transfers between devices, resample_whole(): oldest = ppermute(oldest, 'dom', perm=pages)  5.28 us
    another operation x5, other arithmetic, on_device(): return jnp.stack(results)  4.42 us
  transfers between devices with their start and end apart: 5, of which 3 were waited for; matrix products, arithmetic and copies ran while one was open for 22% of the time, Pallas kernels for 0%

profile of v1, /device:TPU:0, one launch (start us, length us, event | category | flops | bytes accessed | tf_op | source)
XLA Modules:
  0.0 168.3 jit_solution(2464773652439822147)
XLA Ops:
  7.5 3.0 %collective-permute-start = (bf16[2,16,2048]{2,1,0:T(8,128)(2,1)S(1)}, bf16[2,16,2048]{2,1,0:T(8,128)(2,1)}, u32[]{:S(2)}, u32[]{:S(2)}) collective-permute-start(bf16[2,16,2048]{2,1,0:T(8,128)(2,1)S(1)} %reshape.274), channel_id=1, source_target_pairs={{0,2},{2,0},{1,3},{3,1},{4,6},{6,4},{5,7},{7,5},{8,10},{10,8},{9,1... | collective-permute-start | bytes 393224 | tf_op jit(solution)/shard_map/ppermute | solution.py:26
  12.8 4.1 %fusion.120 = (bf16[1,2048,4,128]{3,2,1,0:T(4,128)(2,1)S(1)}, bf16[1,2048,4,128]{3,2,1,0:T(4,128)(2,1)}) fusion(bf16[2,2048,4,128]{3,2,1,0:T(4,128)(2,1)} %param.7), kind=kLoop, calls=%fused_computation.202 | loop fusion | bytes 8388608 | tf_op jit(solution)/shard_map/slice | solution.py:77
  23.9 4.2 %multiply_reduce_fusion = (f32[4,16,8]{2,1,0:T(8,128)}, f32[4,16,8,2048]{3,2,1,0:T(8,128)}) fusion(bf16[1,2048,4,128]{3,2,1,0:T(4,128)(2,1)S(1)} %get-tuple-element.17, bf16[1,16,4,8,128]{4,3,2,1,0:T(8,128)(2,1)} %get-tuple-element.22), kind=kOutput, calls=%fused_computation.4 | convolution fusion | flops 270532096 | bytes 6424576 | tf_op jit(solution)/shard_map/pkgh,tkh->kpgt/dot_general | solution.py:41
  28.1 4.2 %multiply_reduce_fusion.1 = (f32[4,16,8]{2,1,0:T(8,128)}, f32[4,16,8,2048]{3,2,1,0:T(8,128)}) fusion(bf16[1,2048,4,128]{3,2,1,0:T(4,128)(2,1)S(1)} %get-tuple-element.17, bf16[1,16,4,8,128]{4,3,2,1,0:T(8,128)(2,1)} %get-tuple-element.20), kind=kOutput, calls=%fused_computation.5 | convolution fusion | flops 270532096 | bytes 6424576 | tf_op jit(solution)/shard_map/pkgh,tkh->kpgt/dot_general | solution.py:41
  32.3 3.3 %multiply_reduce_fusion.2 = (f32[4,16,8]{2,1,0:T(8,128)}, f32[4,16,8,2048]{3,2,1,0:T(8,128)}) fusion(bf16[1,2048,4,128]{3,2,1,0:T(4,128)(2,1)S(1)} %get-tuple-element.17, bf16[1,16,4,8,128]{4,3,2,1,0:T(8,128)(2,1)S(1)} %copy-done.6), kind=kOutput, calls=%fused_computation.6 | convolution fusion | flops 270532096 | bytes 6424576 | tf_op jit(solution)/shard_map/pkgh,tkh->kpgt/dot_general | solution.py:41
  35.6 3.2 %multiply_reduce_fusion.3 = (f32[4,16,8]{2,1,0:T(8,128)}, f32[4,16,8,2048]{3,2,1,0:T(8,128)}) fusion(bf16[1,2048,4,128]{3,2,1,0:T(4,128)(2,1)S(1)} %get-tuple-element.17, bf16[1,16,4,8,128]{4,3,2,1,0:T(8,128)(2,1)S(1)} %get-tuple-element.19), kind=kOutput, calls=%fused_computation.7 | convolution fusion | flops 270532096 | bytes 6424576 | tf_op jit(solution)/shard_map/pkgh,tkh->kpgt/dot_general | solution.py:41
  39.6 1.1 broadcast_select_fusion.2
  41.1 4.6 %collective-permute-done.1 = bf16[2,16,2048]{2,1,0:T(8,128)(2,1)S(1)} collective-permute-done((bf16[2,16,2048]{2,1,0:T(8,128)(2,1)S(1)}, bf16[2,16,2048]{2,1,0:T(8,128)(2,1)S(1)}, u32[]{:S(2)}, u32[]{:S(2)}) %collective-permute-start.1) | collective-permute-done | bytes 131104 | tf_op jit(solution)/shard_map/ppermute | solution.py:26
  48.4 1.6 fusion.124
  50.0 1.4 bitcast_maximum_fusion.2
  52.9 1.3 broadcast_select_fusion
  54.2 1.8 %collective-permute-start.3 = (bf16[2,16,2048]{2,1,0:T(8,128)(2,1)S(1)}, bf16[2,16,2048]{2,1,0:T(8,128)(2,1)S(1)}, u32[]{:S(2)}, u32[]{:S(2)}) collective-permute-start(bf16[2,16,2048]{2,1,0:T(8,128)(2,1)S(1)} %get-tuple-element.63), channel_id=1, source_target_pairs={{0,2},{2,0},{1,3},{3,1},{4,6},{6,4},{5,7},{7,5},{8,10},{10,8},{9,1... | collective-permute-start | bytes 393224 | tf_op jit(solution)/shard_map/ppermute | solution.py:26
  56.3 2.9 %collective-permute-done.3 = bf16[2,16,2048]{2,1,0:T(8,128)(2,1)S(1)} collective-permute-done((bf16[2,16,2048]{2,1,0:T(8,128)(2,1)S(1)}, bf16[2,16,2048]{2,1,0:T(8,128)(2,1)S(1)}, u32[]{:S(2)}, u32[]{:S(2)}) %collective-permute-start.3) | collective-permute-done | bytes 131104 | tf_op jit(solution)/shard_map/ppermute | solution.py:26
  63.9 22.1 %all-reduce.2 = (f32[16,4,8]{2,0,1:T(8,128)S(1)}, f32[16,4,8]{2,0,1:T(8,128)S(1)}, f32[16,4,8]{2,0,1:T(8,128)S(1)}, f32[16,4,8]{2,0,1:T(8,128)S(1)}) all-reduce(f32[16,4,8]{2,0,1:T(8,128)S(1)} %bitcast_maximum_fusion, f32[16,4,8]{2,0,1:T(8,128)S(1)} %bitcast_maximum_fusion.1, ...), channel_id=1, replica_groups=mesh['groups'=2,'ctx'=4,'dom'=2,'tp'=2] {'ctx'}, use_global_device_ids=true, to_apply=%region_27.28 | all-reduce | flops 2048 | bytes 16384 | tf_op jit(solution)/shard_map/pmax | solution.py:54
  86.1 3.2 %fusion.6 = f32[4,16,8]{2,1,0:T(8,128)S(1)} fusion(f32[4,16,8,2048]{3,2,1,0:T(8,128)} %get-tuple-element.58, f32[4,16,8]{2,1,0:T(8,128)S(1)} %bitcast.230), kind=kLoop, calls=%fused_computation.14 | loop fusion | flops 3145216 | bytes 4198400 | tf_op jit(solution)/shard_map/reduce_sum | solution.py:57
  90.6 1.1 copy-done.2
  93.6 1.3 copy-done.1
  102.6 3.0 %fusion = f32[4,16,8]{2,1,0:T(8,128)S(1)} fusion(f32[4,16,8,2048]{3,2,1,0:T(8,128)} %get-tuple-element.76, f32[4,16,8]{2,1,0:T(8,128)S(1)} %bitcast.225), kind=kLoop, calls=%fused_computation.8 | loop fusion | flops 3145216 | bytes 4198400 | tf_op jit(solution)/shard_map/reduce_sum | solution.py:57
  105.6 22.4 %all-reduce = (f32[16,4,8]{2,0,1:T(8,128)S(1)}, f32[16,4,8]{2,0,1:T(8,128)S(1)}, f32[16,4,8]{2,0,1:T(8,128)S(1)}, f32[16,4,8]{2,0,1:T(8,128)S(1)}) all-reduce(f32[16,4,8]{2,0,1:T(8,128)S(1)} %bitcast_add_fusion, f32[16,4,8]{2,0,1:T(8,128)S(1)} %bitcast_add_fusion.1, ...), channel_id=1, replica_groups=mesh['groups'=2,'ctx'=4,'dom'=2,'tp'=2] {'ctx'}, use_global_device_ids=true, to_apply=%region_31.32 | all-reduce | flops 2048 | bytes 16384 | tf_op jit(solution)/shard_map/psum | solution.py:66
  128.0 28.1 %all-reduce.5.cloned.1.call-done = (f32[16,4,8,128]{3,2,0,1:T(8,128)}, f32[16,4,8,128]{3,2,0,1:T(8,128)}, f32[16,4,8,128]{3,2,0,1:T(8,128)}, f32[16,4,8,128]{3,2,0,1:T(8,128)}) async-done(((f32[16,4,8,128]{3,2,0,1:T(8,128)}, f32[16,4,8,128]{3,2,0,1:T(8,128)}, f32[16,4,8,128]{3,2,0,1:T(8,128)}, f32[16,4,8,128]{3,2,0,1:T(8,128)}), (f32[16,4,8,128]{3,2,0,1:T(8,128)}, f32[16,4,8,128]{3,2,0,1:T(8,128)}, ...) | async-done | bytes 1048592 | tf_op jit(solution)/shard_map/psum | solution.py:66
  156.1 1.1 fusion.63
  157.2 1.1 fusion.62
  158.3 1.1 fusion.61
  159.4 1.1 fusion.60
  (123 shorter events, 32.1 us)
Async XLA Ops:
  6.5 149.5 %all-reduce.5.cloned.1.call-start = ((), (), s32[]{:S(2)}) async-start(), calls=%async_computation | async-start | bytes 2097152 | tf_op jit(solution)/shard_map/psum | solution.py:66
  7.5 32.0 %collective-permute-start = (bf16[2,16,2048]{2,1,0:T(8,128)(2,1)S(1)}, bf16[2,16,2048]{2,1,0:T(8,128)(2,1)}, u32[]{:S(2)}, u32[]{:S(2)}) collective-permute-start(bf16[2,16,2048]{2,1,0:T(8,128)(2,1)S(1)} %reshape.274), channel_id=1, source_target_pairs={{0,2},{2,0},{1,3},{3,1},{4,6},{6,4},{5,7},{7,5},{8,10},{10,8},{9,1... | collective-permute-start | bytes 393224 | tf_op jit(solution)/shard_map/ppermute | solution.py:26
  12.8 4.1 %copy-start.5 = (bf16[4,16,4,8,128]{4,3,2,1,0:T(8,128)(2,1)S(1)}, bf16[4,16,4,8,128]{4,3,2,1,0:T(8,128)(2,1)}, u32[]{:S(2)}) copy-start(bf16[4,16,4,8,128]{4,3,2,1,0:T(8,128)(2,1)} %param.6) | copy-start | bytes 1572868
  12.8 4.9 %copy-start.13 = (bf16[4,2,16,4,128]{4,3,2,1,0:T(4,128)(2,1)S(1)}, bf16[4,2,16,4,128]{4,3,2,1,0:T(4,128)(2,1)}, u32[]{:S(2)}) copy-start(bf16[4,2,16,4,128]{4,3,2,1,0:T(4,128)(2,1)} %param.9) | copy-start | bytes 393220
  18.3 3.4 %copy-start.10 = (bf16[2,16,4,128]{3,2,1,0:T(4,128)(2,1)}, bf16[2,16,4,128]{3,2,1,0:T(4,128)(2,1)S(1)}, u32[]{:S(2)}) copy-start(bf16[2,16,4,128]{3,2,1,0:T(4,128)(2,1)S(1)} %get-tuple-element.32) | copy-start | bytes 98308
  18.3 4.4 %copy-start.11 = (bf16[2,16,4,128]{3,2,1,0:T(4,128)(2,1)}, bf16[2,16,4,128]{3,2,1,0:T(4,128)(2,1)S(1)}, u32[]{:S(2)}) copy-start(bf16[2,16,4,128]{3,2,1,0:T(4,128)(2,1)S(1)} %get-tuple-element.33) | copy-start | bytes 98308
  20.0 1.7 %copy-start.16 = (pred[16,4]{1,0:T(8,128)(4,1)}, pred[16,4]{1,0:T(8,128)(4,1)S(1)}, u32[]{:S(2)}) copy-start(pred[16,4]{1,0:T(8,128)(4,1)S(1)} %get-tuple-element.53) | copy-start | bytes 196
  20.0 1.7 %copy-start.18 = (pred[16,4]{1,0:T(8,128)(4,1)}, pred[16,4]{1,0:T(8,128)(4,1)S(1)}, u32[]{:S(2)}) copy-start(pred[16,4]{1,0:T(8,128)(4,1)S(1)} %get-tuple-element.51) | copy-start | bytes 196
  20.0 2.7 %copy-start.17 = (pred[16,4]{1,0:T(8,128)(4,1)}, pred[16,4]{1,0:T(8,128)(4,1)S(1)}, u32[]{:S(2)}) copy-start(pred[16,4]{1,0:T(8,128)(4,1)S(1)} %get-tuple-element.44) | copy-start | bytes 196
  28.1 4.2 %copy-start.6 = (bf16[1,16,4,8,128]{4,3,2,1,0:T(8,128)(2,1)S(1)}, bf16[1,16,4,8,128]{4,3,2,1,0:T(8,128)(2,1)}, u32[]{:S(2)}) copy-start(bf16[1,16,4,8,128]{4,3,2,1,0:T(8,128)(2,1)} %get-tuple-element.21) | copy-start | bytes 393220
  38.9 12.5 %copy-start.19 = (pred[16,4]{1,0:T(8,128)(4,1)S(1)}, pred[16,4]{1,0:T(8,128)(4,1)}, u32[]{:S(2)}) copy-start(pred[16,4]{1,0:T(8,128)(4,1)} %get-tuple-element.43) | copy-start | bytes 196
  38.9 13.4 %copy-start.12 = (f32[4,16,8]{2,1,0:T(8,128)S(1)}, f32[4,16,8]{2,1,0:T(8,128)}, u32[]{:S(2)}) copy-start(f32[4,16,8]{2,1,0:T(8,128)} %get-tuple-element.75) | copy-start | bytes 6148
  40.7 5.0 %collective-permute-start.1 = (bf16[2,16,2048]{2,1,0:T(8,128)(2,1)S(1)}, bf16[2,16,2048]{2,1,0:T(8,128)(2,1)S(1)}, u32[]{:S(2)}, u32[]{:S(2)}) collective-permute-start(bf16[2,16,2048]{2,1,0:T(8,128)(2,1)S(1)} %get-tuple-element.59), channel_id=1, source_target_pairs={{0,2},{2,0},{1,3},{3,1},{4,6},{6,4},{5,7},{7,5},{8,10},{10,8},{9,1... | collective-permute-start | bytes 393224 | tf_op jit(solution)/shard_map/ppermute | solution.py:26
  46.7 6.1 %collective-permute-start.2 = (bf16[2,16,2048]{2,1,0:T(8,128)(2,1)S(1)}, bf16[2,16,2048]{2,1,0:T(8,128)(2,1)}, u32[]{:S(2)}, u32[]{:S(2)}) collective-permute-start(bf16[2,16,2048]{2,1,0:T(8,128)(2,1)S(1)} %get-tuple-element.61), channel_id=1, source_target_pairs={{0,2},{2,0},{1,3},{3,1},{4,6},{6,4},{5,7},{7,5},{8,10},{10,8},{9,1... | collective-permute-start | bytes 393224 | tf_op jit(solution)/shard_map/ppermute | solution.py:26
  48.4 3.9 %copy-start.7 = (bf16[2,16,4,4,128]{4,2,3,1,0:T(4,128)(2,1)}, bf16[2,16,4,4,128]{4,2,3,1,0:T(4,128)(2,1)S(1)}, u32[]{:S(2)}) copy-start(bf16[2,16,4,4,128]{4,2,3,1,0:T(4,128)(2,1)S(1)} %get-tuple-element.81) | copy-start | bytes 393220
  52.9 36.4 %copy-start.4 = (bf16[1,2048,4,128]{3,2,1,0:T(4,128)(2,1)S(1)}, bf16[1,2048,4,128]{3,2,1,0:T(4,128)(2,1)}, u32[]{:S(2)}) copy-start(bf16[1,2048,4,128]{3,2,1,0:T(4,128)(2,1)} %get-tuple-element.18) | copy-start | bytes 6291460
  54.2 5.0 %collective-permute-start.3 = (bf16[2,16,2048]{2,1,0:T(8,128)(2,1)S(1)}, bf16[2,16,2048]{2,1,0:T(8,128)(2,1)S(1)}, u32[]{:S(2)}, u32[]{:S(2)}) collective-permute-start(bf16[2,16,2048]{2,1,0:T(8,128)(2,1)S(1)} %get-tuple-element.63), channel_id=1, source_target_pairs={{0,2},{2,0},{1,3},{3,1},{4,6},{6,4},{5,7},{7,5},{8,10},{10,8},{9,1... | collective-permute-start | bytes 393224 | tf_op jit(solution)/shard_map/ppermute | solution.py:26
  86.1 3.5 %copy-start.3 = (f32[4,16,8,2048]{3,2,1,0:T(8,128)S(1)}, f32[4,16,8,2048]{3,2,1,0:T(8,128)}, u32[]{:S(2)}) copy-start(f32[4,16,8,2048]{3,2,1,0:T(8,128)} %get-tuple-element.58) | copy-start | bytes 12582916
  89.5 2.2 %copy-start.2 = (f32[4,16,8,2048]{3,2,1,0:T(8,128)S(1)}, f32[4,16,8,2048]{3,2,1,0:T(8,128)}, u32[]{:S(2)}) copy-start(f32[4,16,8,2048]{3,2,1,0:T(8,128)} %get-tuple-element.68) | copy-start | bytes 12582916
  92.8 2.2 %copy-start.1 = (f32[4,16,8,2048]{3,2,1,0:T(8,128)S(1)}, f32[4,16,8,2048]{3,2,1,0:T(8,128)}, u32[]{:S(2)}) copy-start(f32[4,16,8,2048]{3,2,1,0:T(8,128)} %get-tuple-element.72) | copy-start | bytes 12582916
  96.0 3.1 %copy-start.15 = (f32[16,4,8,4]{2,3,1,0:T(4,128)S(1)}, f32[16,4,8,4]{2,3,1,0:T(4,128)}, u32[]{:S(2)}) copy-start(f32[16,4,8,4]{2,3,1,0:T(4,128)} %get-tuple-element.74) | copy-start | bytes 24580
  96.0 3.3 %copy-start.8 = (bf16[2,16,4,4,128]{4,2,3,1,0:T(4,128)(2,1)S(1)}, bf16[2,16,4,4,128]{4,2,3,1,0:T(4,128)(2,1)}, u32[]{:S(2)}) copy-start(bf16[2,16,4,4,128]{4,2,3,1,0:T(4,128)(2,1)} %copy-done.7) | copy-start | bytes 393220
  96.0 4.2 %copy-start = (f32[4,16,8,2048]{3,2,1,0:T(8,128)S(1)}, f32[4,16,8,2048]{3,2,1,0:T(8,128)}, u32[]{:S(2)}) copy-start(f32[4,16,8,2048]{3,2,1,0:T(8,128)} %get-tuple-element.76) | copy-start | bytes 12582916
  100.3 1.1 copy-start.14
  (1 other events, 0.6 us)
Sparse Core Ops, SparseCore 0:
  102.6 53.3 all-reduce.4
